TPU v7x, 32 devices: a whole 2x2x4 slice. The times are simulated.
32 devices in a mesh: section: 2 (over core), ctx: 8 (over z, x), tp: 2 (over y).
Axes of the slice: x: 2, y: 2, z: 4, core: 2. Of those that a mesh axis runs over, the one named last changes fastest.
Arguments:
- layer_input: bfloat16 [2, 1024, 1024], P(None, 'ctx'), may hold values from -6 to 6
- cotangent: bfloat16 [2, 1024, 1024], P(None, 'ctx'), may hold values from -6 to 6
- w_qkv: bfloat16 [2, 1024, 3, 1024], P('section', None, None, 'tp'), may hold values from -0.1875 to 0.1875
- b_qv: bfloat16 [2, 2, 1024], P('section', None, 'tp'), may hold values from -3 to 3
- w_out: bfloat16 [2, 1024, 1024], P('section', 'tp'), may hold values from -4 to 4
- b_out: bfloat16 [2, 1024], P('section'), may hold values from -3 to 3
- w_fc: bfloat16 [2, 1024, 4096], P('section', None, 'tp'), may hold values from -0.1875 to 0.1875
- b_fc: bfloat16 [2, 4096], P('section', 'tp'), may hold values from -3 to 3
- w_proj: bfloat16 [2, 4096, 1024], P('section', 'tp'), may hold values from -0.09375 to 0.09375
- b_proj: bfloat16 [2, 1024], P('section'), may hold values from -3 to 3
- ln_gain: float32 [2, 2, 1024], P('section'), may hold values from 0.5 to 1.5
- ln_bias: float32 [2, 2, 1024], P('section'), may hold values from -3 to 3
Outputs:
- activations: bfloat16 [2, 2, 1024, 1024], P('section', None, 'ctx')
- input_grads: float32 [2, 2, 1024, 1024], P('section', None, 'ctx')
- grad_w_qkv: float32 [2, 1024, 3, 1024], P('section', None, None, 'tp')
- grad_b_qv: float32 [2, 2, 1024], P('section', None, 'tp')
- grad_w_out: float32 [2, 1024, 1024], P('section', 'tp')
- grad_b_out: float32 [2, 1024], P('section')
- grad_w_fc: float32 [2, 1024, 4096], P('section', None, 'tp')
- grad_b_fc: float32 [2, 4096], P('section', 'tp')
- grad_w_proj: float32 [2, 4096, 1024], P('section', 'tp')
- grad_b_proj: float32 [2, 1024], P('section')
- grad_ln_gain: float32 [2, 2, 1024], P('section')
- grad_ln_bias: float32 [2, 2, 1024], P('section')
All inputs are finite; a program needn't handle non-finite values.
Results may differ from a plain program's by a relative error of at most 0.028.
Values may be sent and summed in bfloat16 or wider, within the bound.
A program may use at most 192 MiB of HBM per device.

v0:
```python
import jax
import jax.numpy as jnp
from jax import lax
from jax.sharding import PartitionSpec as P

HD = 64
EPS = 1e-05
GELU_C = 0.7978845608028654


def shifted(value, axis, steps):
    count = lax.axis_size(axis)
    first, last = (max(0, -steps), min(count, count - steps))
    return lax.ppermute(value, axis, [(source, source + steps) for source in range(first, last)])


def norm_forward(values, gain_vec, shift_vec):
    row_mean = jnp.mean(values, axis=-1, keepdims=True)
    centered = values - row_mean
    inv_std = lax.rsqrt(jnp.mean(centered * centered, axis=-1, keepdims=True) + EPS)
    normed = centered * inv_std
    return (normed * gain_vec + shift_vec, normed, inv_std)


def norm_backward(upstream, normed, inv_std, gain_vec):
    dnormed = upstream * gain_vec
    centered_grad = (
        dnormed
        - jnp.mean(dnormed, axis=-1, keepdims=True)
        - normed * jnp.mean(dnormed * normed, axis=-1, keepdims=True)
    )
    return (inv_std * centered_grad, jnp.sum(upstream * normed, axis=0), jnp.sum(upstream, axis=0))


def gelu_parts(pre_act):
    tanh_val = jnp.tanh(GELU_C * (pre_act + 0.044715 * pre_act * pre_act * pre_act))
    gelu_value = 0.5 * pre_act * (1.0 + tanh_val)
    gelu_slope = 0.5 * (1.0 + tanh_val) + 0.5 * pre_act * (1.0 - tanh_val * tanh_val) * GELU_C * (
        1.0 + 3.0 * 0.044715 * pre_act * pre_act
    )
    return (gelu_value, gelu_slope)


def split_heads(values, head_count):
    return values.reshape(values.shape[0], head_count, values.shape[1] // head_count)


def fold_keys(running, block_kv, queries, query_pos, head_count):
    totals, accum = running
    key_rows, val_rows = block_kv
    head_q = split_heads(queries, head_count)
    head_k = split_heads(key_rows, head_count)
    head_v = split_heads(val_rows, head_count)
    score_scale = HD ** (-0.5)
    scores = (
        jnp.einsum("qhd,khd->hqk", head_q, head_k, preferred_element_type=jnp.float32) * score_scale
    )
    key_pos = jnp.arange(key_rows.shape[0], dtype=jnp.int32)
    causal = query_pos[:, None] >= key_pos[None, :]
    weights = jnp.where(causal[None], jnp.exp(scores), 0.0)
    totals = jnp.sum(weights, axis=-1).T
    portion = jnp.einsum(
        "hqk,khd->qhd", weights.astype(jnp.bfloat16), head_v, preferred_element_type=jnp.float32
    )
    return (totals, portion.reshape(accum.shape))


def layer_forward(layer_in, weights_set, query_pos):
    w_qkv, b_qv, w_out, b_out, w_fc, b_fc, w_proj, b_proj, ln_gain, ln_bias = weights_set
    row_count, model_width = layer_in.shape
    local_cols = w_qkv.shape[2]
    head_count = local_cols // HD
    layer_f32 = layer_in.astype(jnp.float32)
    first_norm, normed_a, inv_a = norm_forward(layer_f32, ln_gain[0], ln_bias[0])
    first_bf = first_norm.astype(jnp.bfloat16)
    joined = jnp.dot(
        first_bf, w_qkv.reshape(model_width, 3 * local_cols), preferred_element_type=jnp.float32
    )
    queries = (joined[:, :local_cols] + b_qv[0].astype(jnp.float32)).astype(jnp.bfloat16)
    key_rows = joined[:, local_cols : 2 * local_cols].astype(jnp.bfloat16)
    val_rows = (joined[:, 2 * local_cols :] + b_qv[1].astype(jnp.float32)).astype(jnp.bfloat16)
    init_state = (
        jnp.zeros((row_count, head_count), jnp.float32),
        jnp.zeros((row_count, local_cols), jnp.float32),
    )
    totals, accum = fold_keys(
        init_state,
        (
            lax.all_gather(key_rows, "ctx", axis=0, tiled=True),
            lax.all_gather(val_rows, "ctx", axis=0, tiled=True),
        ),
        queries,
        query_pos,
        head_count,
    )
    held_keys = (key_rows, val_rows)
    attended = (
        (accum.reshape(row_count, head_count, HD) / totals[:, :, None])
        .reshape(row_count, local_cols)
        .astype(jnp.bfloat16)
    )
    log_total = jnp.log(totals)
    attn_mixed = lax.psum(
        jnp.dot(attended, w_out, preferred_element_type=jnp.float32).astype(jnp.bfloat16), "tp"
    ).astype(jnp.float32)
    hidden_in = layer_f32 + attn_mixed + b_out.astype(jnp.float32)
    second_norm, normed_b, inv_b = norm_forward(hidden_in, ln_gain[1], ln_bias[1])
    second_bf = second_norm.astype(jnp.bfloat16)
    pre_act = jnp.dot(second_bf, w_fc, preferred_element_type=jnp.float32) + b_fc.astype(
        jnp.float32
    )
    gelu_value, gelu_slope = gelu_parts(pre_act)
    act_bf = gelu_value.astype(jnp.bfloat16)
    mlp_mixed = lax.psum(
        jnp.dot(act_bf, w_proj, preferred_element_type=jnp.float32).astype(jnp.bfloat16), "tp"
    ).astype(jnp.float32)
    result = hidden_in + mlp_mixed + b_proj.astype(jnp.float32)
    saved = (
        normed_a,
        inv_a,
        first_bf,
        queries,
        (key_rows, val_rows),
        held_keys,
        attended,
        log_total,
        normed_b,
        inv_b,
        second_bf,
        act_bf,
        gelu_slope,
    )
    return (result.astype(jnp.bfloat16), saved)


def layer_backward(upstream, saved, weights_set, query_pos):
    w_qkv, b_qv, w_out, b_out, w_fc, b_fc, w_proj, b_proj, ln_gain, ln_bias = weights_set
    (
        normed_a,
        inv_a,
        first_bf,
        queries,
        own_kv,
        held_keys,
        attended,
        log_total,
        normed_b,
        inv_b,
        second_bf,
        act_bf,
        gelu_slope,
    ) = saved
    row_count, model_width = upstream.shape
    local_cols = w_qkv.shape[2]
    head_count = local_cols // HD
    score_scale = HD ** (-0.5)
    up_bf = upstream.astype(jnp.bfloat16)
    grad_b_proj = jnp.sum(upstream, axis=0)
    grad_w_proj = jnp.dot(act_bf.T, up_bf, preferred_element_type=jnp.float32)
    d_pre = jnp.dot(up_bf, w_proj.T, preferred_element_type=jnp.float32) * gelu_slope
    d_pre_bf = d_pre.astype(jnp.bfloat16)
    grad_b_fc = jnp.sum(d_pre, axis=0)
    grad_w_fc = jnp.dot(second_bf.T, d_pre_bf, preferred_element_type=jnp.float32)
    d_second = lax.psum(
        jnp.dot(d_pre_bf, w_fc.T, preferred_element_type=jnp.float32).astype(jnp.bfloat16), "tp"
    ).astype(jnp.float32)
    d_hidden_ln, gain_b, shift_b = norm_backward(d_second, normed_b, inv_b, ln_gain[1])
    d_hidden = upstream + d_hidden_ln
    grad_b_out = jnp.sum(d_hidden, axis=0)
    hidden_bf = d_hidden.astype(jnp.bfloat16)
    grad_w_out = jnp.dot(attended.T, hidden_bf, preferred_element_type=jnp.float32)
    d_attended = jnp.dot(hidden_bf, w_out.T, preferred_element_type=jnp.float32).astype(
        jnp.bfloat16
    )
    all_keys, all_vals = (
        lax.all_gather(held_keys[0], "ctx", axis=0, tiled=True),
        lax.all_gather(held_keys[1], "ctx", axis=0, tiled=True),
    )
    head_q = split_heads(queries, head_count)
    head_k = split_heads(all_keys, head_count)
    head_v = split_heads(all_vals, head_count)
    head_d = split_heads(d_attended, head_count)
    scores = (
        jnp.einsum("qhd,khd->hqk", head_q, head_k, preferred_element_type=jnp.float32) * score_scale
    )
    key_pos = jnp.arange(all_keys.shape[0], dtype=jnp.int32)
    causal = query_pos[:, None] >= key_pos[None, :]
    probs = jnp.where(causal[None], jnp.exp(scores - log_total.T[:, :, None]), 0.0)
    row_delta = jnp.sum(
        d_attended.astype(jnp.float32).reshape(row_count, head_count, HD)
        * attended.astype(jnp.float32).reshape(row_count, head_count, HD),
        axis=-1,
    )
    d_probs = jnp.einsum("qhd,khd->hqk", head_d, head_v, preferred_element_type=jnp.float32)
    d_scores = (probs * (d_probs - row_delta.T[:, :, None])).astype(jnp.bfloat16)
    d_query = (
        jnp.einsum("hqk,khd->qhd", d_scores, head_k, preferred_element_type=jnp.float32).reshape(
            row_count, local_cols
        )
        * score_scale
    )
    key_term = (
        jnp.einsum("hqk,qhd->khd", d_scores, head_q, preferred_element_type=jnp.float32).reshape(
            all_keys.shape[0], local_cols
        )
        * score_scale
    )
    val_term = jnp.einsum(
        "hqk,qhd->khd", probs.astype(jnp.bfloat16), head_d, preferred_element_type=jnp.float32
    ).reshape(all_keys.shape[0], local_cols)
    d_key, d_val = (
        lax.psum_scatter(
            key_term.astype(jnp.bfloat16), "ctx", scatter_dimension=0, tiled=True
        ).astype(jnp.float32),
        lax.psum_scatter(
            val_term.astype(jnp.bfloat16), "ctx", scatter_dimension=0, tiled=True
        ).astype(jnp.float32),
    )
    grad_b_qv = jnp.stack([jnp.sum(d_query, axis=0), jnp.sum(d_val, axis=0)])
    d_joined = jnp.concatenate([d_query, d_key, d_val], axis=1).astype(jnp.bfloat16)
    grad_w_qkv = jnp.dot(first_bf.T, d_joined, preferred_element_type=jnp.float32).reshape(
        model_width, 3, local_cols
    )
    d_first = lax.psum(
        jnp.dot(
            d_joined,
            w_qkv.reshape(model_width, 3 * local_cols).T,
            preferred_element_type=jnp.float32,
        ).astype(jnp.bfloat16),
        "tp",
    ).astype(jnp.float32)
    d_in_ln, gain_a, shift_a = norm_backward(d_first, normed_a, inv_a, ln_gain[0])
    d_input = d_hidden + d_in_ln
    grads = (
        grad_w_qkv,
        grad_b_qv,
        grad_w_out,
        grad_b_out,
        grad_w_fc,
        grad_b_fc,
        grad_w_proj,
        grad_b_proj,
        jnp.stack([gain_a, gain_b]),
        jnp.stack([shift_a, shift_b]),
    )
    return (d_input, grads)


def body(
    layer_input, cotangent, w_qkv, b_qv, w_out, b_out, w_fc, b_fc, w_proj, b_proj, ln_gain, ln_bias
):
    weights_set = (
        w_qkv[0],
        b_qv[0],
        w_out[0],
        b_out[0],
        w_fc[0],
        b_fc[0],
        w_proj[0],
        b_proj[0],
        ln_gain[0],
        ln_bias[0],
    )
    later_segment = lax.axis_index("section") == 1
    micro, row_count, model_width = layer_input.shape
    query_pos = lax.axis_index("ctx") * row_count + jnp.arange(row_count, dtype=jnp.int32)
    incoming = jnp.zeros((row_count, model_width), jnp.bfloat16)
    results = []
    saved_ticks = []
    for tick_index in range(micro + 1):
        if tick_index < micro:
            fresh_input = layer_input[tick_index]
        else:
            fresh_input = jnp.zeros((row_count, model_width), jnp.bfloat16)
        layer_in = jnp.where(later_segment, incoming, fresh_input)
        result, saved = layer_forward(layer_in, weights_set, query_pos)
        results.append(result)
        saved_ticks.append(saved)
        if tick_index < micro:
            incoming = shifted(result, "section", 1)
    outgoing = jnp.zeros((row_count, model_width), jnp.float32)
    grad_totals = []
    input_grads_all = []
    for tick_index in range(micro + 1):
        if tick_index < micro:
            given_grad = cotangent[tick_index].astype(jnp.float32)
        else:
            given_grad = jnp.zeros((row_count, model_width), jnp.float32)
        upstream = jnp.where(later_segment, given_grad, outgoing)
        saved = jax.tree.map(
            lambda late_val, early_val: jnp.where(later_segment, late_val, early_val),
            saved_ticks[min(tick_index + 1, micro)],
            saved_ticks[max(tick_index - 1, 0)],
        )
        d_input, grads = layer_backward(upstream, saved, weights_set, query_pos)
        if tick_index == 0:
            grad_totals = grads
        else:
            grad_totals = jax.tree.map(jnp.add, grad_totals, grads)
        input_grads_all.append(d_input)
        if tick_index < micro:
            outgoing = shifted(d_input.astype(jnp.bfloat16), "section", -1).astype(d_input.dtype)
    activations = jnp.stack(
        [
            jnp.where(later_segment, results[batch_index + 1], results[batch_index])
            for batch_index in range(micro)
        ]
    )[None]
    input_grads = jnp.stack(
        [
            jnp.where(later_segment, input_grads_all[batch_index], input_grads_all[batch_index + 1])
            for batch_index in range(micro)
        ]
    )[None]
    summed = (
        lax.psum(grad_totals[0].astype(jnp.bfloat16), "ctx").astype(jnp.float32),
        lax.psum(grad_totals[1].astype(jnp.bfloat16), "ctx").astype(jnp.float32),
        lax.psum(grad_totals[2].astype(jnp.bfloat16), "ctx").astype(jnp.float32),
        lax.psum(grad_totals[3].astype(jnp.bfloat16), "ctx").astype(jnp.float32),
        lax.psum(grad_totals[4].astype(jnp.bfloat16), "ctx").astype(jnp.float32),
        lax.psum(grad_totals[5].astype(jnp.bfloat16), "ctx").astype(jnp.float32),
        lax.psum(grad_totals[6].astype(jnp.bfloat16), "ctx").astype(jnp.float32),
        lax.psum(grad_totals[7].astype(jnp.bfloat16), "ctx").astype(jnp.float32),
        lax.psum(grad_totals[8].astype(jnp.bfloat16), "ctx").astype(jnp.float32),
        lax.psum(grad_totals[9].astype(jnp.bfloat16), "ctx").astype(jnp.float32),
    )
    return (
        activations,
        input_grads,
        summed[0][None],
        summed[1][None],
        summed[2][None],
        summed[3][None],
        summed[4][None],
        summed[5][None],
        summed[6][None],
        summed[7][None],
        summed[8][None],
        summed[9][None],
    )


def solution(mesh):
    placed = (
        P(None, "ctx", None),
        P(None, "ctx", None),
        P("section", None, None, "tp"),
        P("section", None, "tp"),
        P("section", "tp", None),
        P("section", None),
        P("section", None, "tp"),
        P("section", "tp"),
        P("section", "tp", None),
        P("section", None),
        P("section", None, None),
        P("section", None, None),
    )
    return jax.shard_map(
        body,
        mesh=mesh,
        in_specs=placed,
        out_specs=(
            P("section", None, "ctx", None),
            P("section", None, "ctx", None),
            P("section", None, None, "tp"),
            P("section", None, "tp"),
            P("section", "tp", None),
            P("section", None),
            P("section", None, "tp"),
            P("section", "tp"),
            P("section", "tp", None),
            P("section", None),
            P("section", None, None),
            P("section", None, None),
        ),
        check_vma=False,
    )
```

profile of v0, /device:TPU:0, one launch (start us, length us, event | category | flops | bytes accessed | tf_op | source)
XLA Modules:
  0.0 1655.5 jit_solution(18073447266085569030)
XLA Ops:
  21.0 42.0 %all-gather.15.cloned.1.call-done = bf16[1024,512]{1,0:T(8,128)(2,1)} async-done(((bf16[128,512]{1,0:T(8,128)(2,1)}), bf16[1024,512]{1,0:T(8,128)(2,1)}) %all-gather.15.cloned.1.call-update) | async-done | bytes 1048592 | tf_op jit(solution)/shard_map/all_gather | solution.py:89
  69.6 34.5 %all-gather.13.cloned.1.call-done = bf16[1024,512]{1,0:T(8,128)(2,1)} async-done(((bf16[128,512]{1,0:T(8,128)(2,1)}), bf16[1024,512]{1,0:T(8,128)(2,1)}) %all-gather.13.cloned.1.call-update) | async-done | bytes 1048592 | tf_op jit(solution)/shard_map/all_gather | solution.py:90
  109.9 22.1 %all-reduce.16.cloned.1.call-done = bf16[128,1024]{1,0:T(8,128)(2,1)} async-done(((bf16[128,1024]{1,0:T(8,128)(2,1)}), bf16[128,1024]{1,0:T(8,128)(2,1)}) %all-reduce.16.cloned.1.call-update) | async-done | bytes 262160 | tf_op jit(solution)/shard_map/psum | solution.py:103
  139.4 23.4 %all-reduce.18.cloned.1.call-done = bf16[128,1024]{1,0:T(8,128)(2,1)} async-done(((bf16[128,1024]{1,0:T(8,128)(2,1)}), bf16[128,1024]{1,0:T(8,128)(2,1)}) %all-reduce.18.cloned.1.call-update) | async-done | bytes 262160 | tf_op jit(solution)/shard_map/psum | solution.py:114
  173.6 39.7 %all-gather.19.cloned.1.call-done = bf16[1024,512]{1,0:T(8,128)(2,1)} async-done(((bf16[128,512]{1,0:T(8,128)(2,1)}), bf16[1024,512]{1,0:T(8,128)(2,1)}) %all-gather.19.cloned.1.call-update) | async-done | bytes 1048592 | tf_op jit(solution)/shard_map/all_gather | solution.py:89
  220.6 33.7 %all-gather.17.cloned.1.call-done = bf16[1024,512]{1,0:T(8,128)(2,1)} async-done(((bf16[128,512]{1,0:T(8,128)(2,1)}), bf16[1024,512]{1,0:T(8,128)(2,1)}) %all-gather.17.cloned.1.call-update) | async-done | bytes 1048592 | tf_op jit(solution)/shard_map/all_gather | solution.py:90
  261.6 21.6 %all-reduce.20.cloned.1.call-done = bf16[128,1024]{1,0:T(8,128)(2,1)} async-done(((bf16[128,1024]{1,0:T(8,128)(2,1)}), bf16[128,1024]{1,0:T(8,128)(2,1)}) %all-reduce.20.cloned.1.call-update) | async-done | bytes 262160 | tf_op jit(solution)/shard_map/psum | solution.py:103
  297.9 28.0 %all-reduce.34.cloned.1.call-done = (bf16[128,1024]{1,0:T(8,128)(2,1)}, bf16[128,1024]{1,0:T(8,128)(2,1)}) async-done(((bf16[128,1024]{1,0:T(8,128)(2,1)}, bf16[128,1024]{1,0:T(8,128)(2,1)}), (bf16[128,1024]{1,0:T(8,128)(2,1)}, bf16[128,1024]{1,0:T(8,128)(2,1)})) %all-reduce.34.cloned.1.call-update) | async-done | bytes 524304 | tf_op jit(solution)/shard_map/psum | solution.py:164
  338.4 30.5 %all-gather.25.cloned.1.call-done = bf16[1024,512]{1,0:T(8,128)(2,1)} async-done(((bf16[128,512]{1,0:T(8,128)(2,1)}), bf16[1024,512]{1,0:T(8,128)(2,1)}) %all-gather.25.cloned.1.call-update) | async-done | bytes 1048592 | tf_op jit(solution)/shard_map/all_gather | solution.py:176
  381.8 28.1 %all-gather.23.cloned.1.call-done = bf16[1024,512]{1,0:T(8,128)(2,1)} async-done(((bf16[128,512]{1,0:T(8,128)(2,1)}), bf16[1024,512]{1,0:T(8,128)(2,1)}) %all-gather.23.cloned.1.call-update) | async-done | bytes 1048592 | tf_op jit(solution)/shard_map/all_gather | solution.py:89
  422.1 28.9 %all-gather.27.cloned.1.call-done = bf16[1024,512]{1,0:T(8,128)(2,1)} async-done(((bf16[128,512]{1,0:T(8,128)(2,1)}), bf16[1024,512]{1,0:T(8,128)(2,1)}) %all-gather.27.cloned.1.call-update) | async-done | bytes 1048592 | tf_op jit(solution)/shard_map/all_gather | solution.py:177
  464.2 27.8 %all-gather.21.cloned.1.call-done = bf16[1024,512]{1,0:T(8,128)(2,1)} async-done(((bf16[128,512]{1,0:T(8,128)(2,1)}), bf16[1024,512]{1,0:T(8,128)(2,1)}) %all-gather.21.cloned.1.call-update) | async-done | bytes 1048592 | tf_op jit(solution)/shard_map/all_gather | solution.py:90
  500.4 58.6 %reduce-scatter.21.cloned.1.call-done = bf16[128,512]{1,0:T(8,128)(2,1)} async-done(((bf16[1024,512]{1,0:T(8,128)(2,1)}), bf16[128,512]{1,0:T(8,128)(2,1)}) %reduce-scatter.21.cloned.1.call-update) | async-done | bytes 131088
  560.1 65.4 %reduce-scatter.19.cloned.1.call-done = bf16[128,512]{1,0:T(8,128)(2,1)} async-done(((bf16[1024,512]{1,0:T(8,128)(2,1)}), bf16[128,512]{1,0:T(8,128)(2,1)}) %reduce-scatter.19.cloned.1.call-update) | async-done | bytes 131088
  631.6 26.0 %all-reduce.32.cloned.1.call-done = (bf16[128,1024]{1,0:T(8,128)(2,1)}, bf16[128,1024]{1,0:T(8,128)(2,1)}) async-done(((bf16[128,1024]{1,0:T(8,128)(2,1)}, bf16[128,1024]{1,0:T(8,128)(2,1)}), (bf16[128,1024]{1,0:T(8,128)(2,1)}, bf16[128,1024]{1,0:T(8,128)(2,1)})) %all-reduce.32.cloned.1.call-update) | async-done | bytes 524304 | tf_op jit(solution)/shard_map/psum | solution.py:224
  677.7 22.7 %all-gather.29.cloned.1.call-done = bf16[1024,512]{1,0:T(8,128)(2,1)} async-done(((bf16[128,512]{1,0:T(8,128)(2,1)}), bf16[1024,512]{1,0:T(8,128)(2,1)}) %all-gather.29.cloned.1.call-update) | async-done | bytes 1048592 | tf_op jit(solution)/shard_map/all_gather | solution.py:176
  706.7 18.5 %all-reduce.22.cloned.1.call-done = bf16[128,1024]{1,0:T(8,128)(2,1)} async-done(((bf16[128,1024]{1,0:T(8,128)(2,1)}), bf16[128,1024]{1,0:T(8,128)(2,1)}) %all-reduce.22.cloned.1.call-update) | async-done | bytes 262160 | tf_op jit(solution)/shard_map/psum | solution.py:164
  738.7 28.7 %all-gather.31.cloned.1.call-done = bf16[1024,512]{1,0:T(8,128)(2,1)} async-done(((bf16[128,512]{1,0:T(8,128)(2,1)}), bf16[1024,512]{1,0:T(8,128)(2,1)}) %all-gather.31.cloned.1.call-update) | async-done | bytes 1048592 | tf_op jit(solution)/shard_map/all_gather | solution.py:177
  795.2 13.4 all-gather.33.cloned.1.call-done
  810.9 38.7 %all-gather.35.cloned.1.call-done = bf16[1024,512]{1,0:T(8,128)(2,1)} async-done(((bf16[128,512]{1,0:T(8,128)(2,1)}), bf16[1024,512]{1,0:T(8,128)(2,1)}) %all-gather.35.cloned.1.call-update) | async-done | bytes 1048592 | tf_op jit(solution)/shard_map/all_gather | solution.py:177
  858.3 57.7 %reduce-scatter.25.cloned.1.call-done = bf16[128,512]{1,0:T(8,128)(2,1)} async-done(((bf16[1024,512]{1,0:T(8,128)(2,1)}), bf16[128,512]{1,0:T(8,128)(2,1)}) %reduce-scatter.25.cloned.1.call-update) | async-done | bytes 131088
  917.6 65.0 %reduce-scatter.23.cloned.1.call-done = bf16[128,512]{1,0:T(8,128)(2,1)} async-done(((bf16[1024,512]{1,0:T(8,128)(2,1)}), bf16[128,512]{1,0:T(8,128)(2,1)}) %reduce-scatter.23.cloned.1.call-update) | async-done | bytes 131088
  993.1 17.1 %all-reduce.24.cloned.1.call-done = bf16[128,1024]{1,0:T(8,128)(2,1)} async-done(((bf16[128,1024]{1,0:T(8,128)(2,1)}), bf16[128,1024]{1,0:T(8,128)(2,1)}) %all-reduce.24.cloned.1.call-update) | async-done | bytes 262160 | tf_op jit(solution)/shard_map/psum | solution.py:224
  1033.3 17.6 %all-reduce.26.cloned.1.call-done = bf16[128,1024]{1,0:T(8,128)(2,1)} async-done(((bf16[128,1024]{1,0:T(8,128)(2,1)}), bf16[128,1024]{1,0:T(8,128)(2,1)}) %all-reduce.26.cloned.1.call-update) | async-done | bytes 262160 | tf_op jit(solution)/shard_map/psum | solution.py:164
  1084.5 9.6 fusion.30
  1094.1 9.2 fusion.31
  1107.2 22.2 %reduce-scatter.29.cloned.1.call-done = bf16[128,512]{1,0:T(8,128)(2,1)} async-done(((bf16[1024,512]{1,0:T(8,128)(2,1)}), bf16[128,512]{1,0:T(8,128)(2,1)}) %reduce-scatter.29.cloned.1.call-update) | async-done | bytes 131088
  1130.5 65.4 %reduce-scatter.27.cloned.1.call-done = bf16[128,512]{1,0:T(8,128)(2,1)} async-done(((bf16[1024,512]{1,0:T(8,128)(2,1)}), bf16[128,512]{1,0:T(8,128)(2,1)}) %reduce-scatter.27.cloned.1.call-update) | async-done | bytes 131088
  1200.3 7.5 add_convert_fusion.2
  1230.8 39.5 %all-reduce = (bf16[1,2,512]{2,1,0:T(2,128)(2,1)S(1)}, bf16[1,1024]{1,0:T(2,128)(2,1)S(1)}, bf16[1,2048]{1,0:T(2,128)(2,1)S(1)}, bf16[1,1024]{1,0:T(2,128)(2,1)S...) all-reduce(bf16[1,2,512]{2,1,0:T(2,128)(2,1)S(1)} %fusion.327, ...), channel_id=1, replica_groups=mesh['section'=2,'ctx'=8,'tp'=2] {'ctx'}, use_global_device_ids=true, to_apply=%region_55.56 | all-reduce | flops 9216 | bytes 36864 | tf_op jit(solution)/shard_map/psum | solution.py:317
  1279.3 349.7 %all-reduce.28.cloned.1.call-done = (bf16[1,1024,3,512]{1,3,2,0:T(8,128)(2,1)}, bf16[1,512,1024]{2,1,0:T(8,128)(2,1)}, bf16[1,1024,2048]{2,1,0:T(8,128)(2,1)}, bf16[1,2048,1024]{2,1,0:T(8,128)(2,1)}) async-done(((bf16[1,1024,3,512]{1,3,2,0:T(8,128)(2,1)}, bf16[1,512,1024]{2,1,0:T(8,128)(2,1)}, bf16[1,1024,2048]{2,1,0:T(8,128)(2,1)}, bf16[1,2048,1024]{2,1,0:T(8,128)(2,1)}), ...) | async-done | bytes 12582928 | tf_op jit(solution)/shard_map/psum | solution.py:316
  1637.2 6.8 broadcast_in_dim.177
  (557 shorter events, 339.2 us)
Async XLA Ops:
  7.2 55.7 %all-gather.15.cloned.1.call-start = ((), (), s32[]{:S(2)}) async-start(), calls=%async_computation.7 | async-start | bytes 1179648 | tf_op jit(solution)/shard_map/all_gather | solution.py:89
  19.8 84.3 %all-gather.13.cloned.1.call-start = ((), (), s32[]{:S(2)}) async-start(), calls=%async_computation.6 | async-start | bytes 1179648 | tf_op jit(solution)/shard_map/all_gather | solution.py:90
  20.6 111.3 %all-reduce.16.cloned.1.call-start = ((), (), s32[]{:S(2)}) async-start(), calls=%async_computation.8 | async-start | bytes 524288 | tf_op jit(solution)/shard_map/psum | solution.py:103
  109.8 53.0 %all-reduce.18.cloned.1.call-start = ((), (), s32[]{:S(2)}) async-start(), calls=%async_computation.9 | async-start | bytes 524288 | tf_op jit(solution)/shard_map/psum | solution.py:114
  139.4 73.9 %all-gather.19.cloned.1.call-start = ((), (), s32[]{:S(2)}) async-start(), calls=%async_computation.11 | async-start | bytes 1179648 | tf_op jit(solution)/shard_map/all_gather | solution.py:89
  163.9 2.4 collective-permute-start
  172.8 81.4 %all-gather.17.cloned.1.call-start = ((), (), s32[]{:S(2)}) async-start(), calls=%async_computation.10 | async-start | bytes 1179648 | tf_op jit(solution)/shard_map/all_gather | solution.py:90
  173.4 109.8 %all-reduce.20.cloned.1.call-start = ((), (), s32[]{:S(2)}) async-start(), calls=%async_computation.12 | async-start | bytes 524288 | tf_op jit(solution)/shard_map/psum | solution.py:103
  261.0 64.9 %all-reduce.34.cloned.1.call-start = ((), (), s32[]{:S(2)}) async-start(), calls=%async_computation.33 | async-start | bytes 1048576 | tf_op jit(solution)/shard_map/psum | solution.py:164
  297.1 71.8 %all-gather.25.cloned.1.call-start = ((), (), s32[]{:S(2)}) async-start(), calls=%async_computation.15 | async-start | bytes 1179648 | tf_op jit(solution)/shard_map/all_gather | solution.py:176
  297.8 112.1 %all-gather.23.cloned.1.call-start = ((), (), s32[]{:S(2)}) async-start(), calls=%async_computation.14 | async-start | bytes 1179648 | tf_op jit(solution)/shard_map/all_gather | solution.py:89
  327.8 2.7 collective-permute-start.1
  336.6 114.4 %all-gather.27.cloned.1.call-start = ((), (), s32[]{:S(2)}) async-start(), calls=%async_computation.16 | async-start | bytes 1179648 | tf_op jit(solution)/shard_map/all_gather | solution.py:177
  337.4 154.7 %all-gather.21.cloned.1.call-start = ((), (), s32[]{:S(2)}) async-start(), calls=%async_computation.13 | async-start | bytes 1179648 | tf_op jit(solution)/shard_map/all_gather | solution.py:90
  375.2 183.8 %reduce-scatter.21.cloned.1.call-start = ((), (), s32[]{:S(2)}) async-start(), calls=%async_computation.25 | async-start | bytes 1179648
  421.9 203.6 %reduce-scatter.19.cloned.1.call-start = ((), (), s32[]{:S(2)}) async-start(), calls=%async_computation.24 | async-start | bytes 1179648
  464.2 193.4 %all-reduce.32.cloned.1.call-start = ((), (), s32[]{:S(2)}) async-start(), calls=%async_computation.32 | async-start | bytes 1048576 | tf_op jit(solution)/shard_map/psum | solution.py:224
  629.8 70.6 %all-gather.29.cloned.1.call-start = ((), (), s32[]{:S(2)}) async-start(), calls=%async_computation.18 | async-start | bytes 1179648 | tf_op jit(solution)/shard_map/all_gather | solution.py:176
  631.5 93.6 %all-reduce.22.cloned.1.call-start = ((), (), s32[]{:S(2)}) async-start(), calls=%async_computation.17 | async-start | bytes 524288 | tf_op jit(solution)/shard_map/psum | solution.py:164
  663.0 6.9 collective-permute-start.2
  675.4 92.1 %all-gather.31.cloned.1.call-start = ((), (), s32[]{:S(2)}) async-start(), calls=%async_computation.19 | async-start | bytes 1179648 | tf_op jit(solution)/shard_map/all_gather | solution.py:177
  676.1 132.5 %all-gather.33.cloned.1.call-start = ((), (), s32[]{:S(2)}) async-start(), calls=%async_computation.22 | async-start | bytes 1179648 | tf_op jit(solution)/shard_map/all_gather | solution.py:176
  676.9 172.7 %all-gather.35.cloned.1.call-start = ((), (), s32[]{:S(2)}) async-start(), calls=%async_computation.23 | async-start | bytes 1179648 | tf_op jit(solution)/shard_map/all_gather | solution.py:177
  677.5 238.5 %reduce-scatter.25.cloned.1.call-start = ((), (), s32[]{:S(2)}) async-start(), calls=%async_computation.27 | async-start | bytes 1179648
  738.7 243.9 %reduce-scatter.23.cloned.1.call-start = ((), (), s32[]{:S(2)}) async-start(), calls=%async_computation.26 | async-start | bytes 1179648
  780.6 229.5 %all-reduce.24.cloned.1.call-start = ((), (), s32[]{:S(2)}) async-start(), calls=%async_computation.20 | async-start | bytes 524288 | tf_op jit(solution)/shard_map/psum | solution.py:224
  987.7 63.3 %all-reduce.26.cloned.1.call-start = ((), (), s32[]{:S(2)}) async-start(), calls=%async_computation.21 | async-start | bytes 524288 | tf_op jit(solution)/shard_map/psum | solution.py:164
  1015.3 5.3 collective-permute-start.3
  1026.7 102.7 %reduce-scatter.29.cloned.1.call-start = ((), (), s32[]{:S(2)}) async-start(), calls=%async_computation.29 | async-start | bytes 1179648
  1065.1 130.8 %reduce-scatter.27.cloned.1.call-start = ((), (), s32[]{:S(2)}) async-start(), calls=%async_computation.28 | async-start | bytes 1179648
  1084.3 143.6 %all-reduce.30.cloned.1.call-start = ((), (), s32[]{:S(2)}) async-start(), calls=%async_computation.31 | async-start | bytes 1048576 | tf_op jit(solution)/shard_map/psum | solution.py:114
  1200.2 428.9 %all-reduce.28.cloned.1.call-start = ((), (), s32[]{:S(2)}) async-start(), calls=%async_computation.30 | async-start | bytes 25165824 | tf_op jit(solution)/shard_map/psum | solution.py:316
  (153 other events, 3767.6 us)
Sparse Core Ops, SparseCore 0:
  19.9 42.9 all-gather.14
  65.1 38.9 all-gather.12
  109.9 21.9 all-reduce.15
  139.5 23.2 all-reduce.17
  173.0 40.2 all-gather.18
  215.3 38.9 all-gather.16
  261.2 21.9 all-reduce.19
  297.2 28.6 all-reduce.33
  328.6 40.2 all-gather.24
  370.9 38.9 all-gather.22
  412.0 38.9 all-gather.26
  453.0 38.9 all-gather.20
  496.0 62.9 reduce-scatter.20
  562.3 63.1 reduce-scatter.18
  629.9 27.6 all-reduce.31
  660.1 40.2 all-gather.28
  703.1 21.9 all-reduce.21
  727.1 40.2 all-gather.30
  769.6 38.9 all-gather.32
  810.6 38.9 all-gather.34
  853.0 62.8 reduce-scatter.24
  919.3 63.2 reduce-scatter.22
  987.8 22.3 all-reduce.23
  1026.8 24.0 all-reduce.25
  1065.2 64.1 reduce-scatter.28
  1132.7 63.1 reduce-scatter.26
  1200.3 27.6 all-reduce.29
  1233.9 395.0 all-reduce.27
where the time goes:
time: 1670 us; the launch traced here: 1660 us
  waiting for transfers between devices  1240 us (74%)
  matrix products  188 us (11%)
  local copies, waits for them, and re-layouts  87.3 us (5%)
  other arithmetic  77.7 us (5%)
  blocking collectives  39.5 us (2%)
    psum x1, waiting for transfers between devices, body(): lax.psum(grad_totals[0].astype(jnp.bfloat16), 'ctx').astype(jnp.float32)  350 us
    unnamed x34, waiting for transfers between devices  338 us
    all_gather x3, waiting for transfers between devices, layer_forward(): lax.all_gather(key_rows, 'ctx', axis=0, tiled=True)  110 us
    all_gather x3, waiting for transfers between devices, layer_backward(): lax.all_gather(held_keys[1], 'ctx', axis=0, tiled=True)  96.4 us
    all_gather x3, waiting for transfers between devices, layer_forward(): lax.all_gather(val_rows, 'ctx', axis=0, tiled=True)  96 us
    all_gather x3, waiting for transfers between devices, layer_backward(): lax.all_gather(held_keys[0], 'ctx', axis=0, tiled=True)  66.6 us
    psum x3, waiting for transfers between devices, layer_backward(): lax.psum(jnp.dot(d_pre_bf, w_fc.T, preferred_element_type=jnp.float32).as...  64.1 us
    psum x2, waiting for transfers between devices, layer_forward(): lax.psum(jnp.dot(attended, w_out, preferred_element_type=jnp.float32).ast...  43.7 us
  transfers between devices with their start and end apart: 32, of which 30 were waited for; matrix products, arithmetic and copies ran while one was open for 14% of the time, Pallas kernels for 0%

commit v1 on v0

--- a/solution.py
+++ b/solution.py
@@ -6,6 +6,13 @@
 HD = 64
 EPS = 1e-05
 GELU_C = 0.7978845608028654
+
+
+def all_by_exchange(x, mesh_axis, along):
+    size = lax.axis_size(mesh_axis)
+    pieces = jnp.stack([x for _ in range(size)])
+    pieces = lax.all_to_all(pieces, mesh_axis, split_axis=0, concat_axis=0)
+    return jnp.concatenate(pieces, axis=along)
 
 
 def shifted(value, axis, steps):
@@ -85,10 +92,7 @@
     )
     totals, accum = fold_keys(
         init_state,
-        (
-            lax.all_gather(key_rows, "ctx", axis=0, tiled=True),
-            lax.all_gather(val_rows, "ctx", axis=0, tiled=True),
-        ),
+        (all_by_exchange(key_rows, "ctx", 0), lax.all_gather(val_rows, "ctx", axis=0, tiled=True)),
         queries,
         query_pos,
         head_count,

time: 1670 us -> 1580 us (0.946)
  waiting for transfers between devices: 1240 us -> 1130 us
  starting transfers between devices: 8.31 us -> 26.7 us
    all_gather x3 -> x0, waiting for transfers between devices: 110 us -> none  [layer_forward(): lax.all_gather(key_rows, 'ctx', axis=0, tiled=True)]
    all_to_all x0 -> x3, waiting for transfers between devices: none -> 56.2 us  [all_by_exchange(): pieces = lax.all_to_all(pieces, mesh_axis, split_axis=0, concat_axis=0)]
    all_gather x3, waiting for transfers between devices: 96 us -> 51.3 us  [layer_forward(): lax.all_gather(val_rows, 'ctx', axis=0, tiled=True)]
    all_to_all x0 -> x3, starting transfers between devices: none -> 18.3 us  [all_by_exchange(): pieces = lax.all_to_all(pieces, mesh_axis, split_axis=0, concat_axis=0)]
    unnamed x320 -> x330, local copies, waits for them, and re-layouts: 42.3 us -> 43.2 us
    unnamed x34 -> x31, waiting for transfers between devices: 338 us -> 337 us
  transfers between devices with their start and end apart: 32 -> 32, of which waited for: 30 -> 29; matrix products, arithmetic and copies ran while one was open for 14% -> 15% of each run, Pallas kernels for 0% -> 0%
where the time goes in v1:
time: 1580 us; the launch traced here: 1570 us
  waiting for transfers between devices  1130 us (72%)
  matrix products  187 us (12%)
  local copies, waits for them, and re-layouts  97.5 us (6%)
  other arithmetic  78 us (5%)
  blocking collectives  38.9 us (2%)
  starting transfers between devices  26.7 us (2%)
  between operations  16.1 us (1%)
    psum x1, waiting for transfers between devices, body(): lax.psum(grad_totals[0].astype(jnp.bfloat16), 'ctx').astype(jnp.float32)  350 us
    unnamed x31, waiting for transfers between devices  337 us
    all_gather x3, waiting for transfers between devices, layer_backward(): lax.all_gather(held_keys[1], 'ctx', axis=0, tiled=True)  81.1 us
    all_gather x3, waiting for transfers between devices, layer_backward(): lax.all_gather(held_keys[0], 'ctx', axis=0, tiled=True)  71 us
    psum x3, waiting for transfers between devices, layer_backward(): lax.psum(jnp.dot(d_pre_bf, w_fc.T, preferred_element_type=jnp.float32).as...  64 us
    all_to_all x3, waiting for transfers between devices, all_by_exchange(): pieces = lax.all_to_all(pieces, mesh_axis, split_axis=0, concat_axis=0)  56.2 us
    all_gather x3, waiting for transfers between devices, layer_forward(): lax.all_gather(val_rows, 'ctx', axis=0, tiled=True)  51.3 us
    psum x2, waiting for transfers between devices, layer_forward(): lax.psum(jnp.dot(attended, w_out, preferred_element_type=jnp.float32).ast...  44.2 us
  transfers between devices with their start and end apart: 32, of which 29 were waited for; matrix products, arithmetic and copies ran while one was open for 15% of the time, Pallas kernels for 0%

profile of v1, /device:TPU:0, one launch (start us, length us, event | category | flops | bytes accessed | tf_op | source)
XLA Modules:
  0.0 1573.4 jit_solution(1017605978704812551)
XLA Ops:
  21.2 7.3 all-to-all-start
  30.7 27.7 %all-to-all-done = bf16[8,128,512]{1,2,0:T(8,128)(2,1)S(1)} async-done(((bf16[8,128,512]{1,2,0:T(8,128)(2,1)}), bf16[8,128,512]{1,2,0:T(8,128)(2,1)S(1)}, u32[]{:S(2)}, u32[]{:S(2)}) %all-to-all-start) | async-done | bytes 1048608 | tf_op jit(solution)/shard_map/all_to_all | solution.py:14
  64.7 13.4 all-gather.10.cloned.1.call-done
  83.9 22.0 %all-reduce.16.cloned.1.call-done = bf16[128,1024]{1,0:T(8,128)(2,1)} async-done(((bf16[128,1024]{1,0:T(8,128)(2,1)}), bf16[128,1024]{1,0:T(8,128)(2,1)}) %all-reduce.16.cloned.1.call-update) | async-done | bytes 262160 | tf_op jit(solution)/shard_map/psum | solution.py:107
  113.4 23.4 %all-reduce.18.cloned.1.call-done = bf16[128,1024]{1,0:T(8,128)(2,1)} async-done(((bf16[128,1024]{1,0:T(8,128)(2,1)}), bf16[128,1024]{1,0:T(8,128)(2,1)}) %all-reduce.18.cloned.1.call-update) | async-done | bytes 262160 | tf_op jit(solution)/shard_map/psum | solution.py:118
  155.7 28.5 %all-to-all-done.1 = bf16[8,128,512]{1,2,0:T(8,128)(2,1)} async-done(((bf16[8,128,512]{1,2,0:T(8,128)(2,1)}), bf16[8,128,512]{1,2,0:T(8,128)(2,1)}, u32[]{:S(2)}, u32[]{:S(2)}) %all-to-all-start.1) | async-done | bytes 1048608 | tf_op jit(solution)/shard_map/all_to_all | solution.py:14
  194.5 9.0 all-gather.12.cloned.1.call-done
  210.2 22.1 %all-reduce.20.cloned.1.call-done = bf16[128,1024]{1,0:T(8,128)(2,1)} async-done(((bf16[128,1024]{1,0:T(8,128)(2,1)}), bf16[128,1024]{1,0:T(8,128)(2,1)}) %all-reduce.20.cloned.1.call-update) | async-done | bytes 262160 | tf_op jit(solution)/shard_map/psum | solution.py:107
  247.1 28.0 %all-reduce.34.cloned.1.call-done = (bf16[128,1024]{1,0:T(8,128)(2,1)}, bf16[128,1024]{1,0:T(8,128)(2,1)}) async-done(((bf16[128,1024]{1,0:T(8,128)(2,1)}, bf16[128,1024]{1,0:T(8,128)(2,1)}), (bf16[128,1024]{1,0:T(8,128)(2,1)}, bf16[128,1024]{1,0:T(8,128)(2,1)})) %all-reduce.34.cloned.1.call-update) | async-done | bytes 524304 | tf_op jit(solution)/shard_map/psum | solution.py:168
  292.9 35.1 %all-gather.16.cloned.1.call-done = bf16[1024,512]{1,0:T(8,128)(2,1)} async-done(((bf16[128,512]{1,0:T(8,128)(2,1)}), bf16[1024,512]{1,0:T(8,128)(2,1)}) %all-gather.16.cloned.1.call-update) | async-done | bytes 1048592 | tf_op jit(solution)/shard_map/all_gather | solution.py:180
  355.4 13.7 all-gather.18.cloned.1.call-done
  381.3 28.9 %all-gather.14.cloned.1.call-done = bf16[1024,512]{1,0:T(8,128)(2,1)} async-done(((bf16[128,512]{1,0:T(8,128)(2,1)}), bf16[1024,512]{1,0:T(8,128)(2,1)}) %all-gather.14.cloned.1.call-update) | async-done | bytes 1048592 | tf_op jit(solution)/shard_map/all_gather | solution.py:95
  418.6 58.5 %reduce-scatter.21.cloned.1.call-done = bf16[128,512]{1,0:T(8,128)(2,1)} async-done(((bf16[1024,512]{1,0:T(8,128)(2,1)}), bf16[128,512]{1,0:T(8,128)(2,1)}) %reduce-scatter.21.cloned.1.call-update) | async-done | bytes 131088
  478.1 65.7 %reduce-scatter.19.cloned.1.call-done = bf16[128,512]{1,0:T(8,128)(2,1)} async-done(((bf16[1024,512]{1,0:T(8,128)(2,1)}), bf16[128,512]{1,0:T(8,128)(2,1)}) %reduce-scatter.19.cloned.1.call-update) | async-done | bytes 131088
  549.9 26.0 %all-reduce.32.cloned.1.call-done = (bf16[128,1024]{1,0:T(8,128)(2,1)}, bf16[128,1024]{1,0:T(8,128)(2,1)}) async-done(((bf16[128,1024]{1,0:T(8,128)(2,1)}, bf16[128,1024]{1,0:T(8,128)(2,1)}), (bf16[128,1024]{1,0:T(8,128)(2,1)}, bf16[128,1024]{1,0:T(8,128)(2,1)})) %all-reduce.32.cloned.1.call-update) | async-done | bytes 524304 | tf_op jit(solution)/shard_map/psum | solution.py:228
  595.9 23.0 %all-gather.20.cloned.1.call-done = bf16[1024,512]{1,0:T(8,128)(2,1)} async-done(((bf16[128,512]{1,0:T(8,128)(2,1)}), bf16[1024,512]{1,0:T(8,128)(2,1)}) %all-gather.20.cloned.1.call-update) | async-done | bytes 1048592 | tf_op jit(solution)/shard_map/all_gather | solution.py:180
  625.1 18.5 %all-reduce.22.cloned.1.call-done = bf16[128,1024]{1,0:T(8,128)(2,1)} async-done(((bf16[128,1024]{1,0:T(8,128)(2,1)}), bf16[128,1024]{1,0:T(8,128)(2,1)}) %all-reduce.22.cloned.1.call-update) | async-done | bytes 262160 | tf_op jit(solution)/shard_map/psum | solution.py:168
  657.1 28.7 %all-gather.22.cloned.1.call-done = bf16[1024,512]{1,0:T(8,128)(2,1)} async-done(((bf16[128,512]{1,0:T(8,128)(2,1)}), bf16[1024,512]{1,0:T(8,128)(2,1)}) %all-gather.22.cloned.1.call-update) | async-done | bytes 1048592 | tf_op jit(solution)/shard_map/all_gather | solution.py:181
  714.0 12.9 all-gather.24.cloned.1.call-done
  729.2 38.7 %all-gather.26.cloned.1.call-done = bf16[1024,512]{1,0:T(8,128)(2,1)} async-done(((bf16[128,512]{1,0:T(8,128)(2,1)}), bf16[1024,512]{1,0:T(8,128)(2,1)}) %all-gather.26.cloned.1.call-update) | async-done | bytes 1048592 | tf_op jit(solution)/shard_map/all_gather | solution.py:181
  776.5 57.6 %reduce-scatter.25.cloned.1.call-done = bf16[128,512]{1,0:T(8,128)(2,1)} async-done(((bf16[1024,512]{1,0:T(8,128)(2,1)}), bf16[128,512]{1,0:T(8,128)(2,1)}) %reduce-scatter.25.cloned.1.call-update) | async-done | bytes 131088
  835.8 64.9 %reduce-scatter.23.cloned.1.call-done = bf16[128,512]{1,0:T(8,128)(2,1)} async-done(((bf16[1024,512]{1,0:T(8,128)(2,1)}), bf16[128,512]{1,0:T(8,128)(2,1)}) %reduce-scatter.23.cloned.1.call-update) | async-done | bytes 131088
  910.7 17.4 %all-reduce.24.cloned.1.call-done = bf16[128,1024]{1,0:T(8,128)(2,1)} async-done(((bf16[128,1024]{1,0:T(8,128)(2,1)}), bf16[128,1024]{1,0:T(8,128)(2,1)}) %all-reduce.24.cloned.1.call-update) | async-done | bytes 262160 | tf_op jit(solution)/shard_map/psum | solution.py:228
  951.5 17.5 %all-reduce.26.cloned.1.call-done = bf16[128,1024]{1,0:T(8,128)(2,1)} async-done(((bf16[128,1024]{1,0:T(8,128)(2,1)}), bf16[128,1024]{1,0:T(8,128)(2,1)}) %all-reduce.26.cloned.1.call-update) | async-done | bytes 262160 | tf_op jit(solution)/shard_map/psum | solution.py:168
  1002.5 9.6 fusion.30
  1012.2 9.2 fusion.31
  1025.2 22.3 %reduce-scatter.29.cloned.1.call-done = bf16[128,512]{1,0:T(8,128)(2,1)} async-done(((bf16[1024,512]{1,0:T(8,128)(2,1)}), bf16[128,512]{1,0:T(8,128)(2,1)}) %reduce-scatter.29.cloned.1.call-update) | async-done | bytes 131088
  1048.5 65.6 %reduce-scatter.27.cloned.1.call-done = bf16[128,512]{1,0:T(8,128)(2,1)} async-done(((bf16[1024,512]{1,0:T(8,128)(2,1)}), bf16[128,512]{1,0:T(8,128)(2,1)}) %reduce-scatter.27.cloned.1.call-update) | async-done | bytes 131088
  1118.5 7.6 add_convert_fusion.2
  1149.0 38.9 %all-reduce = (bf16[1,2,512]{2,1,0:T(2,128)(2,1)S(1)}, bf16[1,1024]{1,0:T(2,128)(2,1)S(1)}, bf16[1,2048]{1,0:T(2,128)(2,1)S(1)}, bf16[1,1024]{1,0:T(2,128)(2,1)S...) all-reduce(bf16[1,2,512]{2,1,0:T(2,128)(2,1)S(1)} %fusion.327, ...), channel_id=1, replica_groups=mesh['section'=2,'ctx'=8,'tp'=2] {'ctx'}, use_global_device_ids=true, to_apply=%region_55.56 | all-reduce | flops 9216 | bytes 36864 | tf_op jit(solution)/shard_map/psum | solution.py:321
  1196.9 350.4 %all-reduce.28.cloned.1.call-done = (bf16[1,1024,3,512]{1,3,2,0:T(8,128)(2,1)}, bf16[1,512,1024]{2,1,0:T(8,128)(2,1)}, bf16[1,1024,2048]{2,1,0:T(8,128)(2,1)}, bf16[1,2048,1024]{2,1,0:T(8,128)(2,1)}) async-done(((bf16[1,1024,3,512]{1,3,2,0:T(8,128)(2,1)}, bf16[1,512,1024]{2,1,0:T(8,128)(2,1)}, bf16[1,1024,2048]{2,1,0:T(8,128)(2,1)}, bf16[1,2048,1024]{2,1,0:T(8,128)(2,1)}), ...) | async-done | bytes 12582928 | tf_op jit(solution)/shard_map/psum | solution.py:320
  1555.4 6.8 broadcast_in_dim.177
  (573 shorter events, 358.5 us)
Async XLA Ops:
  21.2 37.2 %all-to-all-start = ((bf16[8,128,512]{1,2,0:T(8,128)(2,1)}), bf16[8,128,512]{1,2,0:T(8,128)(2,1)S(1)}, u32[]{:S(2)}, u32[]{:S(2)}) async-start(bf16[8,128,512]{1,2,0:T(8,128)(2,1)} %stack.132), calls=%async_computation | async-start | bytes 2097152 | tf_op jit(solution)/shard_map/all_to_all | solution.py:14
  28.5 49.7 %all-gather.10.cloned.1.call-start = ((), (), s32[]{:S(2)}) async-start(), calls=%async_computation.9 | async-start | bytes 1179648 | tf_op jit(solution)/shard_map/all_gather | solution.py:95
  30.3 75.7 %all-reduce.16.cloned.1.call-start = ((), (), s32[]{:S(2)}) async-start(), calls=%async_computation.10 | async-start | bytes 524288 | tf_op jit(solution)/shard_map/psum | solution.py:107
  83.8 53.0 %all-reduce.18.cloned.1.call-start = ((), (), s32[]{:S(2)}) async-start(), calls=%async_computation.11 | async-start | bytes 524288 | tf_op jit(solution)/shard_map/psum | solution.py:118
  138.0 2.4 collective-permute-start
  148.1 36.2 %all-to-all-start.1 = ((bf16[8,128,512]{1,2,0:T(8,128)(2,1)}), bf16[8,128,512]{1,2,0:T(8,128)(2,1)}, u32[]{:S(2)}, u32[]{:S(2)}) async-start(bf16[8,128,512]{1,2,0:T(8,128)(2,1)} %stack.133), calls=%async_computation.1 | async-start | bytes 2097152 | tf_op jit(solution)/shard_map/all_to_all | solution.py:14
  153.6 49.9 %all-gather.12.cloned.1.call-start = ((), (), s32[]{:S(2)}) async-start(), calls=%async_computation.12 | async-start | bytes 1179648 | tf_op jit(solution)/shard_map/all_gather | solution.py:95
  154.2 78.2 %all-reduce.20.cloned.1.call-start = ((), (), s32[]{:S(2)}) async-start(), calls=%async_computation.13 | async-start | bytes 524288 | tf_op jit(solution)/shard_map/psum | solution.py:107
  210.2 64.9 %all-reduce.34.cloned.1.call-start = ((), (), s32[]{:S(2)}) async-start(), calls=%async_computation.33 | async-start | bytes 1048576 | tf_op jit(solution)/shard_map/psum | solution.py:168
  246.3 81.7 %all-gather.16.cloned.1.call-start = ((), (), s32[]{:S(2)}) async-start(), calls=%async_computation.15 | async-start | bytes 1179648 | tf_op jit(solution)/shard_map/all_gather | solution.py:180
  247.0 122.0 %all-gather.18.cloned.1.call-start = ((), (), s32[]{:S(2)}) async-start(), calls=%async_computation.16 | async-start | bytes 1179648 | tf_op jit(solution)/shard_map/all_gather | solution.py:181
  277.0 2.7 collective-permute-start.1
  287.1 53.2 %all-to-all-start.2 = ((bf16[8,128,512]{1,2,0:T(8,128)(2,1)}), bf16[8,128,512]{1,2,0:T(8,128)(2,1)}, u32[]{:S(2)}, u32[]{:S(2)}) async-start(bf16[8,128,512]{1,2,0:T(8,128)(2,1)} %stack.135), calls=%async_computation.2 | async-start | bytes 2097152 | tf_op jit(solution)/shard_map/all_to_all | solution.py:14
  292.7 117.6 %all-gather.14.cloned.1.call-start = ((), (), s32[]{:S(2)}) async-start(), calls=%async_computation.14 | async-start | bytes 1179648 | tf_op jit(solution)/shard_map/all_gather | solution.py:95
  334.3 142.8 %reduce-scatter.21.cloned.1.call-start = ((), (), s32[]{:S(2)}) async-start(), calls=%async_computation.25 | async-start | bytes 1179648
  355.4 188.5 %reduce-scatter.19.cloned.1.call-start = ((), (), s32[]{:S(2)}) async-start(), calls=%async_computation.24 | async-start | bytes 1179648
  381.3 194.6 %all-reduce.32.cloned.1.call-start = ((), (), s32[]{:S(2)}) async-start(), calls=%async_computation.32 | async-start | bytes 1048576 | tf_op jit(solution)/shard_map/psum | solution.py:228
  548.1 70.7 %all-gather.20.cloned.1.call-start = ((), (), s32[]{:S(2)}) async-start(), calls=%async_computation.18 | async-start | bytes 1179648 | tf_op jit(solution)/shard_map/all_gather | solution.py:180
  549.8 93.8 %all-reduce.22.cloned.1.call-start = ((), (), s32[]{:S(2)}) async-start(), calls=%async_computation.17 | async-start | bytes 524288 | tf_op jit(solution)/shard_map/psum | solution.py:168
  581.3 7.2 collective-permute-start.2
  593.9 92.0 %all-gather.22.cloned.1.call-start = ((), (), s32[]{:S(2)}) async-start(), calls=%async_computation.19 | async-start | bytes 1179648 | tf_op jit(solution)/shard_map/all_gather | solution.py:181
  594.7 132.2 %all-gather.24.cloned.1.call-start = ((), (), s32[]{:S(2)}) async-start(), calls=%async_computation.22 | async-start | bytes 1179648 | tf_op jit(solution)/shard_map/all_gather | solution.py:180
  595.3 172.6 %all-gather.26.cloned.1.call-start = ((), (), s32[]{:S(2)}) async-start(), calls=%async_computation.23 | async-start | bytes 1179648 | tf_op jit(solution)/shard_map/all_gather | solution.py:181
  595.8 238.2 %reduce-scatter.25.cloned.1.call-start = ((), (), s32[]{:S(2)}) async-start(), calls=%async_computation.27 | async-start | bytes 1179648
  657.1 243.5 %reduce-scatter.23.cloned.1.call-start = ((), (), s32[]{:S(2)}) async-start(), calls=%async_computation.26 | async-start | bytes 1179648
  699.1 229.0 %all-reduce.24.cloned.1.call-start = ((), (), s32[]{:S(2)}) async-start(), calls=%async_computation.20 | async-start | bytes 524288 | tf_op jit(solution)/shard_map/psum | solution.py:228
  905.7 63.2 %all-reduce.26.cloned.1.call-start = ((), (), s32[]{:S(2)}) async-start(), calls=%async_computation.21 | async-start | bytes 524288 | tf_op jit(solution)/shard_map/psum | solution.py:168
  933.2 5.3 collective-permute-start.3
  944.7 102.8 %reduce-scatter.29.cloned.1.call-start = ((), (), s32[]{:S(2)}) async-start(), calls=%async_computation.29 | async-start | bytes 1179648
  983.1 131.1 %reduce-scatter.27.cloned.1.call-start = ((), (), s32[]{:S(2)}) async-start(), calls=%async_computation.28 | async-start | bytes 1179648
  1002.2 144.0 %all-reduce.30.cloned.1.call-start = ((), (), s32[]{:S(2)}) async-start(), calls=%async_computation.31 | async-start | bytes 1048576 | tf_op jit(solution)/shard_map/psum | solution.py:118
  1118.4 428.9 %all-reduce.28.cloned.1.call-start = ((), (), s32[]{:S(2)}) async-start(), calls=%async_computation.30 | async-start | bytes 25165824 | tf_op jit(solution)/shard_map/psum | solution.py:320
  (158 other events, 3661.6 us)
Sparse Core Ops, SparseCore 0:
  31.4 46.6 all-gather.9
  84.0 21.9 all-reduce.15
  113.5 23.2 all-reduce.17
  156.8 46.6 all-gather.11
  210.3 21.9 all-reduce.19
  246.4 28.6 all-reduce.33
  277.8 50.1 all-gather.15
  330.1 38.9 all-gather.17
  371.2 38.9 all-gather.13
  414.1 63.0 reduce-scatter.20
  480.5 63.2 reduce-scatter.18
  548.3 27.5 all-reduce.31
  578.6 40.2 all-gather.19
  621.6 21.9 all-reduce.21
  645.6 40.2 all-gather.21
  687.9 38.9 all-gather.23
  728.9 38.9 all-gather.25
  771.1 62.8 reduce-scatter.24
  837.5 63.0 reduce-scatter.22
  905.9 22.2 all-reduce.23
  944.8 24.0 all-reduce.25
  983.2 64.2 reduce-scatter.28
  1050.9 63.2 reduce-scatter.26
  1118.5 27.5 all-reduce.29
  1152.1 395.1 all-reduce.27
